TPU v7x, 128 devices: a whole 4x4x4 slice. The times are simulated.
128 devices in a mesh: seq: 4 (over x), tp: 32 (over y, z, core).
Axes of the slice: x: 4, y: 4, z: 4, core: 2. Of those that a mesh axis runs over, the one named last changes fastest.
Arguments:
- tokens: bfloat16 [2048, 8192], P('seq', 'tp'), may hold values from -6 to 6
- cotangent: bfloat16 [2048, 8192], P('seq', 'tp'), may hold values from -6 to 6
- w_query: bfloat16 [8192, 8192], P(None, 'tp'), may hold values from -0.0625 to 0.0625
- w_key: bfloat16 [8192, 1024], P('tp'), may hold values from -0.0625 to 0.0625
- w_value: bfloat16 [8192, 1024], P('tp'), may hold values from -0.0625 to 0.0625
- mask_query: int32 [128, 128], P(None, 'tp'), may hold values 0 or 1
- mask_key: int32 [128, 16], P('tp'), may hold values 0 or 1
- mask_value: int32 [128, 16], P('tp'), may hold values 0 or 1
- documents: int32 [4, 512], P('seq'), may hold values from 0 to 7, never falling along the last dimension, each value on 1 to 256 neighbouring positions
Outputs:
- attended: bfloat16 [2048, 8192], P('seq', 'tp')
- grad_tokens: bfloat16 [2048, 8192], P('seq', 'tp')
- grad_query: bfloat16 [8192, 8192], P(None, ('tp', 'seq'))
- grad_key: bfloat16 [8192, 1024], P('tp', 'seq')
- grad_value: bfloat16 [8192, 1024], P('tp', 'seq')
Inputs may be any that keep to these rules, and one draw needn't show every extreme that they name: documents never fall along a sequence; each document holds at most 256 tokens.
All inputs are finite; a program needn't handle non-finite values. No bound on the sum of `mask_query` or of `mask_key` or of `mask_value` on one device may be relied on, other than what follows from the above.
Results may differ from a plain program's by a relative error of at most 0.035.
Values may be sent and summed in bfloat16 or wider, within the bound.
A program may use at most 128 MiB of HBM per device.

v0:
```python
import jax
import jax.numpy as jnp
from jax import lax
from jax.sharding import PartitionSpec as P

H = 64
KVH = 8
HD = 128
BLK = 64


def expand(mask):
    return jnp.repeat(jnp.repeat(mask, BLK, axis=0), BLK, axis=1).astype(jnp.bfloat16)


def on_device(
    tokens, cotangent, w_query, w_key, w_value, mask_query, mask_key, mask_value, documents
):
    tp_count = lax.axis_size("tp")
    heads_here = H // tp_count
    group_size = H // KVH
    sub_heads = min(heads_here, group_size)
    slot_count = heads_here // sub_heads
    my_index = lax.axis_index("tp")
    first_slot = my_index * heads_here // group_size
    seq_len = tokens.shape[0]
    query_width = w_query.shape[1]
    kv_width = w_key.shape[1]
    slot_width = slot_count * HD
    score_scale = HD ** (-0.5)
    full_q = expand(mask_query)
    full_k = expand(mask_key)
    full_v = expand(mask_value)
    mq = w_query * full_q
    mkv = jnp.concatenate([w_key * full_k, w_value * full_v], axis=1)
    gathered = lax.all_gather(tokens, "tp", axis=1, tiled=True)
    query = jnp.dot(gathered, mq, preferred_element_type=jnp.float32).astype(jnp.bfloat16)
    kv_part = lax.dot_general(
        mkv, tokens, (((0,), (1,)), ((), ())), preferred_element_type=jnp.float32
    )
    summed = lax.psum(kv_part.astype(jnp.bfloat16), "tp")
    keys = lax.dynamic_slice_in_dim(summed, first_slot * HD, slot_width, 0)
    values = lax.dynamic_slice_in_dim(summed, kv_width + first_slot * HD, slot_width, 0)
    k_heads = jnp.repeat(keys.reshape(slot_count, HD, seq_len), sub_heads, axis=0)
    v_heads = jnp.repeat(values.reshape(slot_count, HD, seq_len), sub_heads, axis=0)
    q_heads = query.reshape(seq_len, heads_here, HD)
    positions = jnp.arange(seq_len)
    doc = documents[0]
    allowed = (doc[:, None] == doc[None, :]) & (positions[None, :] <= positions[:, None])
    scores = (
        jnp.einsum("qhd,hdk->hqk", q_heads, k_heads, preferred_element_type=jnp.float32)
        * score_scale
    )
    weights = jnp.where(allowed[None], jnp.exp(scores), 0.0)
    probs = weights / jnp.sum(weights, axis=-1, keepdims=True)
    probs_low = probs.astype(jnp.bfloat16)
    attended = jnp.einsum("hqk,hdk->qhd", probs_low, v_heads, preferred_element_type=jnp.float32)
    attended = attended.astype(jnp.bfloat16).reshape(seq_len, query_width)
    grad_heads = cotangent.reshape(seq_len, heads_here, HD)
    dv_heads = jnp.einsum("hqk,qhd->hdk", probs_low, grad_heads, preferred_element_type=jnp.float32)
    d_probs = jnp.einsum("qhd,hdk->hqk", grad_heads, v_heads, preferred_element_type=jnp.float32)
    d_scores = probs * (d_probs - jnp.sum(d_probs * probs, axis=-1, keepdims=True)) * score_scale
    d_scores = d_scores.astype(jnp.bfloat16)
    d_query = jnp.einsum("hqk,hdk->qhd", d_scores, k_heads, preferred_element_type=jnp.float32)
    d_query = d_query.astype(jnp.bfloat16).reshape(seq_len, query_width)
    dk_heads = jnp.einsum("hqk,qhd->hdk", d_scores, q_heads, preferred_element_type=jnp.float32)
    dk_slots = dk_heads.reshape(slot_count, sub_heads, HD, seq_len).sum(axis=1).astype(jnp.bfloat16)
    dv_slots = dv_heads.reshape(slot_count, sub_heads, HD, seq_len).sum(axis=1).astype(jnp.bfloat16)
    dx_heads = lax.psum_scatter(
        lax.dot_general(
            mq, d_query, (((1,), (1,)), ((), ())), preferred_element_type=jnp.float32
        ).astype(jnp.bfloat16),
        "tp",
        scatter_dimension=0,
        tiled=True,
    ).astype(jnp.float32)
    placed = jnp.zeros((2, kv_width, seq_len), jnp.float32)
    local_slots = jnp.stack(
        [dk_slots.reshape(slot_width, seq_len), dv_slots.reshape(slot_width, seq_len)]
    ).astype(jnp.float32)
    placed = lax.dynamic_update_slice(placed, local_slots, (0, first_slot * HD, 0))
    dkv_full = (
        lax.psum(placed.astype(jnp.bfloat16), "tp")
        .astype(jnp.float32)
        .reshape(2 * kv_width, seq_len)
        .astype(jnp.bfloat16)
    )
    dx_kv = lax.dot_general(
        mkv, dkv_full, (((1,), (0,)), ((), ())), preferred_element_type=jnp.float32
    )
    grad_tokens = (dx_heads + dx_kv).T.astype(jnp.bfloat16)
    grad_q_local = lax.dot_general(
        gathered, d_query, (((0,), (0,)), ((), ())), preferred_element_type=jnp.float32
    )
    grad_q_local = grad_q_local * full_q.astype(jnp.float32)
    grad_kv_local = lax.dot_general(
        tokens, dkv_full, (((0,), (1,)), ((), ())), preferred_element_type=jnp.float32
    )
    grad_k_local = grad_kv_local[:, :kv_width] * full_k.astype(jnp.float32)
    grad_v_local = grad_kv_local[:, kv_width:] * full_v.astype(jnp.float32)
    sums = (
        lax.psum_scatter(
            grad_q_local.astype(jnp.bfloat16), "seq", scatter_dimension=1, tiled=True
        ).astype(jnp.float32),
        lax.psum_scatter(
            grad_k_local.astype(jnp.bfloat16), "seq", scatter_dimension=1, tiled=True
        ).astype(jnp.float32),
        lax.psum_scatter(
            grad_v_local.astype(jnp.bfloat16), "seq", scatter_dimension=1, tiled=True
        ).astype(jnp.float32),
    )
    return (
        attended,
        grad_tokens,
        sums[0].astype(jnp.bfloat16),
        sums[1].astype(jnp.bfloat16),
        sums[2].astype(jnp.bfloat16),
    )


def solution(mesh):
    in_specs = (
        P("seq", "tp"),
        P("seq", "tp"),
        P(None, "tp"),
        P("tp", None),
        P("tp", None),
        P(None, "tp"),
        P("tp", None),
        P("tp", None),
        P("seq", None),
    )
    out_specs = (
        P("seq", "tp"),
        P("seq", "tp"),
        P(None, ("tp", "seq")),
        P("tp", "seq"),
        P("tp", "seq"),
    )
    return jax.shard_map(
        on_device, mesh=mesh, in_specs=in_specs, out_specs=out_specs, check_vma=False
    )
```

profile of v0, /device:TPU:1, one launch (start us, length us, event | category | flops | bytes accessed | tf_op | source)
XLA Modules:
  0.0 510.9 jit_solution(4479430856302945396)
XLA Ops:
  7.2 0.0 all-reduce.3.cloned.1.call-start
  7.2 1.3 copy.36
  8.5 0.7 convert_element_type.129
  9.2 0.1 copy.35
  9.3 0.1 broadcast_in_dim.42
  9.4 0.1 convert_element_type.130
  9.5 1.2 copy.34
  10.8 0.1 copy.33
  10.8 0.1 broadcast_in_dim.40
  10.9 0.1 convert_element_type.127
  11.0 0.1 bitcast_multiply_fusion.6
  11.1 2.1 convolution_convert_fusion.1
  13.2 0.0 all-reduce.3.cloned.1.call-update
  13.2 0.0 all-gather.2.cloned.1.call-start
  13.3 0.7 all-gather.2.cloned.1.call-update
  14.0 0.0 all-reduce.5.cloned.1.call-start
  14.0 0.0 copy-start.6
  14.1 6.4 %copy.38 = bf16[8192,256]{0,1:T(8,128)(2,1)} copy(bf16[8192,256]{1,0:T(8,128)(2,1)} %param.11) | data formatting | bytes 8388608 | tf_op args[2]
  20.5 0.1 broadcast_in_dim.45
  20.6 0.1 convert_element_type.134
  20.8 0.1 copy.59
  20.9 4.4 bitcast_multiply_fusion
  25.4 0.9 fusion.16
  26.3 98.1 %all-reduce.3.cloned.1.call-done = bf16[2048,512]{1,0:T(8,128)(2,1)} async-done(((bf16[2048,512]{1,0:T(8,128)(2,1)}), bf16[2048,512]{1,0:T(8,128)(2,1)}) %all-reduce.3.cloned.1.call-update) | async-done | bytes 2097168 | tf_op jit(solution)/shard_map/psum | solution.py:41
  124.4 1.6 constant_dynamic-slice_fusion
  126.1 0.8 copy.37
  126.8 1.3 fusion.23
  128.2 57.4 %all-gather.2.cloned.1.call-done = bf16[512,8192]{1,0:T(8,128)(2,1)} async-done(((bf16[512,256]{1,0:T(8,128)(2,1)}), bf16[512,8192]{1,0:T(8,128)(2,1)}) %all-gather.2.cloned.1.call-update) | async-done | bytes 8388624 | tf_op jit(solution)/shard_map/all_gather | solution.py:36
  185.6 7.1 %convolution_convert_fusion.4 = bf16[256,512]{1,0:T(8,128)(2,1)S(1)} fusion(bf16[8192,256]{0,1:T(8,128)(2,1)} %bitcast_multiply_fusion, bf16[512,8192]{1,0:T(8,128)(2,1)} %all-gather.2.cloned.1.call-done), kind=kOutput, calls=%fused_computation.20 | convolution fusion | flops 2147614720 | bytes 12845056 | tf_op jit(solution)/shard_map/dot_general | solution.py:37
  192.6 0.0 copy-start.15
  192.7 0.8 fusion.7
  193.5 1.3 copy-done.16
  194.8 1.4 fusion.12
  196.2 4.6 fusion.13
  200.8 0.1 broadcast_in_dim.48
  201.0 0.8 copy-done.10
  201.7 0.1 copy-done.11
  201.8 1.3 copy-done
  203.2 0.0 all-reduce.5.cloned.1.call-update
  203.2 0.0 reduce-scatter.9.cloned.1.call-start
  203.2 107.1 %all-reduce.5.cloned.1.call-done = bf16[2048,512]{1,0:T(8,128)(2,1)} async-done(((bf16[2048,512]{1,0:T(8,128)(2,1)}), bf16[2048,512]{1,0:T(8,128)(2,1)}) %all-reduce.5.cloned.1.call-update) | async-done | bytes 2097168 | tf_op jit(solution)/shard_map/psum | solution.py:83
  310.3 2.3 convolution_bitcast_fusion.1
  312.6 1.3 fusion.14
  313.9 0.0 reduce-scatter.9.cloned.1.call-update
  313.9 0.0 reduce-scatter.11.cloned.1.call-start
  314.0 5.2 %convolution_convert_fusion.2 = bf16[2,128,512]{2,1,0:T(8,128)(2,1)S(1)} fusion(f32[2,512,512]{2,1,0:T(8,128)} %copy-done.4, bf16[128,512]{1,0:T(8,128)(2,1)S(1)} %copy-done.9, f32[2,512,512]{1,2,0:T(8,128)} %copy-done.16, f32[2,512]{1,0:T(2,128)S(1)} %get-tuple-element.19, pred[512,512]{0,1:T(8,128)(4,1)} %fusion.16), kind=kOutput, calls=%fused_computation.18 | convolution fusion | flops 140117504 | bytes 4853760 | tf_op jit(solution)/shard_map/hqk,hdk->qhd/dot_general | solution.py:64
  319.2 0.0 reduce-scatter.11.cloned.1.call-update
  319.2 0.2 reduce-scatter.5.cloned.1.call-start
  319.4 7.8 %convolution_convert_fusion = bf16[8192,512]{1,0:T(8,128)(2,1)} fusion(bf16[8192,256]{0,1:T(8,128)(2,1)} %bitcast_multiply_fusion, bf16[512,256]{0,1:T(8,128)(2,1)S(1)} %bitcast.91), kind=kOutput, calls=%fused_computation.1 | convolution fusion | flops 2151677952 | bytes 12845056 | tf_op jit(solution)/shard_map/dot_general | solution.py:70
  327.2 0.0 reduce-scatter.5.cloned.1.call-update
  327.3 0.0 reduce-scatter.7.cloned.1.call-start
  327.3 0.5 broadcast_in_dim.46
  327.8 7.8 %fusion.2 = bf16[8192,256]{0,1:T(8,128)(2,1)} fusion(bf16[512,256]{0,1:T(8,128)(2,1)S(1)} %bitcast.92, bf16[512,8192]{1,0:T(8,128)(2,1)} %all-gather.2.cloned.1.call-done, bf16[8192,256]{0,1:T(8,128)(2,1)S(1)} %bitcast.88), kind=kOutput, calls=%fused_computation.4 | convolution fusion | flops 2153775104 | bytes 17039360 | tf_op jit(solution)/shard_map/dot_general | solution.py:92
  335.6 0.0 reduce-scatter.7.cloned.1.call-update
  335.6 0.9 copy-done.5
  336.5 3.2 convolution_convert_fusion.3
  339.7 1.8 copy.48
  341.5 1.7 copy.50
  343.1 13.4 %reduce-scatter.11.cloned.1.call-done = bf16[256,256]{0,1:T(8,128)(2,1)} async-done(((bf16[256,1024]{0,1:T(8,128)(2,1)}), bf16[256,256]{0,1:T(8,128)(2,1)}) %reduce-scatter.11.cloned.1.call-update) | async-done | bytes 131088 | tf_op jit(solution)/shard_map/reduce_scatter | solution.py:108
  356.5 1.7 copy.51
  358.2 95.2 %reduce-scatter.5.cloned.1.call-done = bf16[256,512]{1,0:T(8,128)(2,1)} async-done(((bf16[8192,512]{1,0:T(8,128)(2,1)}), bf16[256,512]{1,0:T(8,128)(2,1)}) %reduce-scatter.5.cloned.1.call-update) | async-done | bytes 262160 | tf_op jit(solution)/shard_map/reduce_scatter | solution.py:69
  453.4 1.7 fusion.9
  455.0 0.8 copy.49
  455.9 48.2 %reduce-scatter.7.cloned.1.call-done = bf16[8192,64]{0,1:T(8,128)(2,1)} async-done(((bf16[8192,256]{0,1:T(8,128)(2,1)}), bf16[8192,64]{0,1:T(8,128)(2,1)}) %reduce-scatter.7.cloned.1.call-update) | async-done | bytes 1048592 | tf_op jit(solution)/shard_map/reduce_scatter | solution.py:102
  (31 shorter events, 0.1 us)
Async XLA Ops:
  7.2 3.6 copy-start.13
  7.2 3.9 copy-start.2
  7.2 117.2 %all-reduce.3.cloned.1.call-start = ((), (), s32[]{:S(2)}) async-start(), calls=%async_computation.4 | async-start | bytes 4194304 | tf_op jit(solution)/shard_map/psum | solution.py:41
  13.2 172.4 %all-gather.2.cloned.1.call-start = ((), (), s32[]{:S(2)}) async-start(), calls=%async_computation.5 | async-start | bytes 8650752 | tf_op jit(solution)/shard_map/all_gather | solution.py:36
  14.0 296.3 %all-reduce.5.cloned.1.call-start = ((), (), s32[]{:S(2)}) async-start(), calls=%async_computation.7 | async-start | bytes 4194304 | tf_op jit(solution)/shard_map/psum | solution.py:83
  14.0 6.4 %copy-start.14 = (s32[128,4]{0,1:T(4,128)S(1)}, s32[128,4]{0,1:T(4,128)}, u32[]{:S(2)}) copy-start(s32[128,4]{0,1:T(4,128)} %param.14) | copy-start | bytes 6148
  14.0 6.7 %copy-start.6 = (bf16[512,256]{1,0:T(8,128)(2,1)S(1)}, bf16[512,256]{1,0:T(8,128)(2,1)}, u32[]{:S(2)}) copy-start(bf16[512,256]{1,0:T(8,128)(2,1)} %param.10) | copy-start | bytes 786436
  20.9 4.5 copy-start.12
  128.1 68.0 %copy-start.4 = (f32[2,512,512]{2,1,0:T(8,128)}, f32[2,512,512]{2,1,0:T(8,128)S(1)}, u32[]{:S(2)}) copy-start(f32[2,512,512]{2,1,0:T(8,128)S(1)} %fusion.23) | copy-start | bytes 6291460
  185.6 7.1 %copy-start.7 = (pred[512,512]{0,1:T(8,128)(4,1)S(1)}, pred[512,512]{0,1:T(8,128)(4,1)}, u32[]{:S(2)}) copy-start(pred[512,512]{0,1:T(8,128)(4,1)} %fusion.16) | copy-start | bytes 786436
  185.6 7.1 %copy-start.8 = (bf16[128,512]{1,0:T(8,128)(2,1)S(1)}, bf16[128,512]{1,0:T(8,128)(2,1)}, u32[]{:S(2)}) copy-start(bf16[128,512]{1,0:T(8,128)(2,1)} %get-tuple-element.17) | copy-start | bytes 393220
  192.6 0.8 copy-start.15
  193.4 1.3 copy-start.16
  200.8 0.9 copy-start.10
  200.8 1.0 copy-start.11
  200.8 109.4 %copy-start.3 = (bf16[512,256]{1,0:T(8,128)(2,1)S(1)}, bf16[512,256]{1,0:T(8,128)(2,1)}, u32[]{:S(2)}) copy-start(bf16[512,256]{1,0:T(8,128)(2,1)} %param.9) | copy-start | bytes 786436
  201.8 1.3 copy-start
  203.2 138.3 %reduce-scatter.9.cloned.1.call-start = ((), (), s32[]{:S(2)}) async-start(), calls=%async_computation.9 | async-start | bytes 655360 | tf_op jit(solution)/shard_map/reduce_scatter | solution.py:105
  312.6 1.4 copy-start.9
  313.9 42.6 %reduce-scatter.11.cloned.1.call-start = ((), (), s32[]{:S(2)}) async-start(), calls=%async_computation.10 | async-start | bytes 655360 | tf_op jit(solution)/shard_map/reduce_scatter | solution.py:108
  319.2 134.2 %reduce-scatter.5.cloned.1.call-start = ((), (), s32[]{:S(2)}) async-start(), calls=%async_computation.6 | async-start | bytes 8650752 | tf_op jit(solution)/shard_map/reduce_scatter | solution.py:69
  327.3 176.8 %reduce-scatter.7.cloned.1.call-start = ((), (), s32[]{:S(2)}) async-start(), calls=%async_computation.8 | async-start | bytes 5242880 | tf_op jit(solution)/shard_map/reduce_scatter | solution.py:102
  335.6 0.9 copy-start.5
  336.5 116.8 %copy-start.1 = (bf16[2048,512]{1,0:T(8,128)(2,1)S(1)}, bf16[2048,512]{1,0:T(8,128)(2,1)}, u32[]{:S(2)}) copy-start(bf16[2048,512]{1,0:T(8,128)(2,1)} %all-reduce.5.cloned.1.call-done) | copy-start | bytes 6291460
Sparse Core Ops, SparseCore 0:
  13.3 111.0 all-reduce.2
  126.6 58.9 all-gather.1
  203.3 106.9 all-reduce.4
  314.0 18.8 reduce-scatter.8
  335.1 21.3 reduce-scatter.10
  360.1 93.2 reduce-scatter.4
  456.3 47.6 reduce-scatter.6
where the time goes:
time: 512 us; the launch traced here: 511 us
  waiting for transfers between devices  420 us (82%)
  matrix products  45.2 us (9%)
  local copies, waits for them, and re-layouts  23.3 us (5%)
  between operations  14.4 us (3%)
  other arithmetic  7.43 us (1%)
    psum x1, waiting for transfers between devices, on_device(): lax.psum(placed.astype(jnp.bfloat16), 'tp').astype(jnp.float32)  107 us
    psum x1, waiting for transfers between devices, on_device(): summed = lax.psum(kv_part.astype(jnp.bfloat16), 'tp')  98.1 us
    reduce_scatter x1, waiting for transfers between devices, on_device(): lax.psum_scatter(lax.dot_general(mq, d_query, (((1,), (1,)), ((), ())), p...  95.2 us
    all_gather x1, waiting for transfers between devices, on_device(): gathered = lax.all_gather(tokens, 'tp', axis=1, tiled=True)  57.4 us
    reduce_scatter x1, waiting for transfers between devices, on_device(): lax.psum_scatter(grad_q_local.astype(jnp.bfloat16), 'seq', scatter_dimens...  48.2 us
    unnamed x41, local copies, waits for them, and re-layouts  19.3 us
    reduce_scatter x1, waiting for transfers between devices, on_device(): lax.psum_scatter(grad_v_local.astype(jnp.bfloat16), 'seq', scatter_dimens...  13.4 us
  transfers between devices with their start and end apart: 7, of which 6 were waited for; matrix products, arithmetic and copies ran while one was open for 9% of the time, Pallas kernels for 0%

commit v1 on v0

v1 whole, which is shorter than its diff:
```python
import functools

import jax
import jax.numpy as jnp
from jax import lax
from jax.experimental import pallas as pl
from jax.experimental.pallas import tpu as pltpu
from jax.sharding import PartitionSpec as P

MESH = pl.DeviceIdType.MESH
F32 = jnp.float32
BF16 = jnp.bfloat16
HD = 128
BLK = 64
L = 512
N_SEMS = 240


def nt(a, b):
    return lax.dot_general(a, b, (((1,), (1,)), ((), ())), preferred_element_type=F32)


def tn(a, b):
    return lax.dot_general(a, b, (((0,), (0,)), ((), ())), preferred_element_type=F32)


def nn(a, b):
    return jnp.dot(a, b, preferred_element_type=F32)


def add_to(ref, idx, *terms):
    total = ref[idx].astype(F32)
    for term in terms:
        total = total + term.astype(F32)
    ref[idx] = total.astype(BF16)


def drive(gens, times=1):
    for _ in range(times):
        for g in gens:
            next(g, None)


def finish(gens):
    live = list(gens)
    while live:
        for g in list(live):
            if next(g, StopIteration) is StopIteration:
                live.remove(g)


class Links:
    def __init__(self, send_sem, recv_sem):
        self.s = lax.axis_index("seq")
        t = lax.axis_index("tp")
        self.y = lax.div(t, 8)
        self.z = lax.rem(lax.div(t, 2), 4)
        self.c = lax.rem(t, 2)
        self.send_sem, self.recv_sem = send_sem, recv_sem
        self.count = 0
        self.sent = []

    def at(self, dx=0, dy=0, dz=0, flip=False):
        x = lax.rem(self.s + (dx + 4), 4)
        y = lax.rem(self.y + (dy + 4), 4)
        z = lax.rem(self.z + (dz + 4), 4)
        c = 1 - self.c if flip else self.c
        return (x, (y * 4 + z) * 2 + c)

    def wrap(self, base, offset):
        return lax.rem(base + (offset + 8), 4)

    def send(self, src, dst, device):
        k = self.count
        self.count += 1
        copy = pltpu.make_async_remote_copy(
            src_ref=src,
            dst_ref=dst,
            send_sem=self.send_sem.at[k],
            recv_sem=self.recv_sem.at[k],
            device_id=device,
            device_id_type=MESH,
        )
        copy.start()
        self.sent.append(copy)
        return copy

    def drain(self):
        for copy in self.sent:
            copy.wait_send()


def gather_half(lk, buf, half, rows, sib):
    h, q = rows // 2, rows // 4
    base = half * h

    def slot(a, b):
        if half == 0:
            return lk.wrap(lk.y, -a), lk.wrap(lk.z, -b)
        return lk.wrap(lk.y, -b), lk.wrap(lk.z, -a)

    def ref(a, b, r0, n):
        yi, zi = slot(a, b)
        return buf.at[yi, zi, lk.c, pl.ds(base + r0, n), :]

    def near(first, step):
        along_y = first == (half == 0)
        return lk.at(dy=step) if along_y else lk.at(dz=step)

    def snd(a, b, r0, n, dev):
        return lk.send(ref(a, b, r0, n), ref(a, b, r0, n), dev)

    def across(a):
        return snd(a, 0, 0, h, near(False, 1)), snd(a, 0, 0, h, near(False, -1))

    def share(a, b):
        sib.append(snd(a, b, 0, h, lk.at(flip=True)))

    far = {}
    up = snd(0, 0, 0, h, near(True, 1))
    down = snd(0, 0, 0, h, near(True, -1))
    yield
    far[0] = across(0)
    yield
    up.wait_recv()
    up2 = snd(1, 0, 0, q, near(True, 1))
    far[1] = across(1)
    share(1, 0)
    yield
    down.wait_recv()
    down2 = snd(-1, 0, q, q, near(True, -1))
    far[-1] = across(-1)
    share(-1, 0)
    yield
    up2.wait_recv()
    down2.wait_recv()
    far[2] = across(2)
    share(2, 0)
    yield
    last = {}
    for a in (0, 1, -1, 2):
        far[a][0].wait_recv()
        one = snd(a, 1, 0, q, near(False, 1))
        share(a, 1)
        yield
        far[a][1].wait_recv()
        last[a] = one, snd(a, -1, q, q, near(False, -1))
        share(a, -1)
        yield
    for a in (0, 1, -1, 2):
        last[a][0].wait_recv()
        last[a][1].wait_recv()
        share(a, 2)
        yield


def scatter_half(lk, buf, half, rows, t1, t2, t3, t4, result):
    h, q = rows // 2, rows // 4
    base = half * h

    def group(a, r0, n):
        if half == 0:
            return buf.at[:, lk.wrap(lk.z, a), pl.ds(base + r0, n), :]
        return buf.at[lk.wrap(lk.y, a), :, pl.ds(base + r0, n), :]

    def idx(a, i, r0, n):
        if half == 0:
            return (i, lk.wrap(lk.z, a), pl.ds(base + r0, n), slice(None))
        return (lk.wrap(lk.y, a), i, pl.ds(base + r0, n), slice(None))

    def one(b, r0, n):
        if half == 0:
            return (lk.wrap(lk.y, b), lk.z, pl.ds(base + r0, n), slice(None))
        return (lk.y, lk.wrap(lk.z, b), pl.ds(base + r0, n), slice(None))

    def near(first, step):
        along_z = first == (half == 0)
        return lk.at(dz=step) if along_z else lk.at(dy=step)

    e1p = lk.send(group(2, 0, q), t1.at[half, 0], near(True, 1))
    e1m = lk.send(group(2, q, q), t1.at[half, 1], near(True, -1))
    yield
    e1p.wait_recv()
    for i in range(4):
        add_to(buf, idx(1, i, 0, q), t1[half, 0, i])
    e2p = lk.send(group(1, 0, h), t2.at[half, 0], near(True, 1))
    yield
    e1m.wait_recv()
    for i in range(4):
        add_to(buf, idx(-1, i, q, q), t1[half, 1, i])
    e2m = lk.send(group(-1, 0, h), t2.at[half, 1], near(True, -1))
    yield
    e2p.wait_recv()
    e2m.wait_recv()
    for i in range(4):
        add_to(buf, idx(0, i, 0, h), t2[half, 0, i], t2[half, 1, i])
    e3p = lk.send(buf.at[one(2, 0, q)], t3.at[half, 0], near(False, 1))
    e3m = lk.send(buf.at[one(2, q, q)], t3.at[half, 1], near(False, -1))
    yield
    e3p.wait_recv()
    add_to(buf, one(1, 0, q), t3[half, 0])
    e4p = lk.send(buf.at[one(1, 0, h)], t4.at[half, 0], near(False, 1))
    e3m.wait_recv()
    add_to(buf, one(-1, q, q), t3[half, 1])
    e4m = lk.send(buf.at[one(-1, 0, h)], t4.at[half, 1], near(False, -1))
    yield
    e4p.wait_recv()
    e4m.wait_recv()
    total = buf[one(0, 0, h)].astype(F32)
    result(base, h, total + t4[half, 0].astype(F32) + t4[half, 1].astype(F32))


class RingSum:
    def __init__(self, lk, buf, relay, final, other, way):
        self.lk, self.buf, self.way = lk, buf, way
        self.relay_buf, self.final_buf, self.other_buf = relay, final, other
        s = lk.s
        self.raw = lk.send(buf.at[lk.wrap(s, 2)], relay, lk.at(dx=way))
        self.direct = lk.send(buf.at[lk.wrap(s, -way)], other, lk.at(dx=-way))

    def relay(self):
        lk = self.lk
        self.raw.wait_recv()
        mine = lk.wrap(lk.s, self.way)
        add_to(self.buf, (mine,), self.relay_buf[...])
        self.done = lk.send(self.buf.at[mine], self.final_buf, lk.at(dx=self.way))

    def result(self):
        self.done.wait_recv()
        self.direct.wait_recv()
        total = self.buf[self.lk.s].astype(F32)
        return total + self.final_buf[...].astype(F32) + self.other_buf[...].astype(F32)


def kernel(
    tok, cot, wq_hbm, wk, wv, mask_q, mask_k, mask_v, docs,
    att, gtok, gq_out, gk_out, gv_out,
    g, mq, mqs, mkv, mw, mws, mexp, mrow, qf, qb, kvp, kvt1, kvt2, kvt3, kvt4, kvh,
    doc_col, dkf, dq, dqs, dqt, tokt, dkvp, dkvt, dkv, dx, dxt1, dxt2, dxt3, dxt4, dxkv,
    gq, gqr, gqf, gqo, gkv, gkvr, gkvf, gkvo,
    send_sem, recv_sem, local_sem,
):
    lk = Links(send_sem, recv_sem)
    y, z, c, s = lk.y, lk.z, lk.c, lk.s
    scale = HD ** (-0.5)
    zp = lax.rem(z, 2)
    z_mate = z + 1 - 2 * zp
    sibling = lk.at(flip=True)
    mate = (s, (y * 4 + z_mate) * 2 + c)
    cross = (s, (y * 4 + z_mate) * 2 + 1 - c)

    weights = pltpu.make_async_copy(wq_hbm, mq, local_sem)
    weights.start()
    barrier = pltpu.get_barrier_semaphore()
    friends = [sibling, cross, lk.at(dy=1), lk.at(dy=-1), lk.at(dz=1), lk.at(dz=-1), lk.at(dx=1), lk.at(dx=-1)]
    for friend in friends:
        pl.semaphore_signal(barrier, inc=1, device_id=friend, device_id_type=MESH)

    lane = lax.div(lax.broadcasted_iota(jnp.int32, (4, 1024), 1), BLK)
    for kind, (w, m) in enumerate(((wk, mask_k), (wv, mask_v))):
        wide = jnp.zeros((4, 1024), F32)
        for j in range(16):
            wide = jnp.where(lane == j, m[:, j : j + 1].astype(F32), wide)
        for b in range(4):
            rows = slice(b * BLK, (b + 1) * BLK)
            masked = (w[rows, :].astype(F32) * wide[b : b + 1, :]).astype(BF16)
            mw[kind, rows, :] = masked
            for head in range(8):
                mkv[head, rows, kind * HD : (kind + 1) * HD] = masked[:, head * HD : (head + 1) * HD]
    g[y, z, c] = tok[...]
    pl.semaphore_wait(barrier, len(friends))

    sib_tok = lk.send(tok, g.at[y, z, c], sibling)
    sib_w = lk.send(mw.at[1 - c], mws, sibling)
    shared = []
    ga = gather_half(lk, g, 0, L, shared)
    gb = gather_half(lk, g, 1, L, shared)
    drive((ga, gb), 2)

    lane = lax.div(lax.broadcasted_iota(jnp.int32, (128, 256), 1), BLK)
    col = lax.broadcasted_iota(jnp.int32, (128, 4), 1)
    wide = jnp.zeros((128, 256), F32)
    for j in range(4):
        wide = jnp.where(lane == j, mask_q[:, j : j + 1].astype(F32), wide)
    mexp[...] = wide
    own_col = jnp.sum(jnp.where(col == s, mask_q[...].astype(F32), 0.0), axis=1, keepdims=True)
    mrow[...] = jnp.broadcast_to(own_col, (128, 128))
    weights.wait()

    def mask_chunk(t, carry):
        yi, zi, ci = lax.div(t, 8), lax.rem(lax.div(t, 2), 4), lax.rem(t, 2)
        for b in range(4):
            rows = slice(b * BLK, (b + 1) * BLK)
            line = mexp[pl.ds(4 * t + b, 1), :]
            mq[yi, zi, ci, rows, :] = (mq[yi, zi, ci, rows, :].astype(F32) * line).astype(BF16)
        return carry

    lax.fori_loop(0, 32, mask_chunk, 0)
    sib_mq = lk.send(mq.at[:, :, 1 - c], mqs, sibling)

    sib_tok.wait_recv()
    sib_w.wait_recv()

    def kv_pair(i, carry):
        cols = pl.ds(pl.multiple_of(i * 256, 256), 256)
        part = nn(tok[...], mw[c, :, cols]) + nn(g[y, z, 1 - c], mws[:, cols])
        part = part.astype(BF16)
        for hh in range(2):
            for th in range(2):
                kvp[i, 2 * hh + th] = part[th * 256 : (th + 1) * 256, hh * HD : (hh + 1) * HD]
        return carry

    lax.fori_loop(0, 4, kv_pair, 0)

    def store_kv(base, n, value):
        kvh[c, zp, base : base + n, :] = value.astype(BF16)

    ka = scatter_half(lk, kvp, 0, 256, kvt1, kvt2, kvt3, kvt4, store_kv)
    kb = scatter_half(lk, kvp, 1, 256, kvt1, kvt2, kvt3, kvt4, store_kv)
    drive((ka, kb))
    drive((ga, gb), 3)
    drive((ka, kb), 2)

    qf[...] = jnp.zeros_like(qf)

    def project(yi, zi, ci):
        qf[...] += nn(g[yi, zi, ci], mq[yi, zi, ci])

    project(y, z, c)
    project(y, z, 1 - c)
    drive((ga, gb), 2)
    drive((ka, kb))
    drive((ga, gb), 2)
    finish((ka, kb))
    hand = [lk.send(kvh.at[c, zp], kvh.at[c, zp], dev) for dev in (sibling, mate, cross)]
    tokt[...] = tok[...].astype(F32).T.astype(BF16)
    finish((ga, gb))

    def project_own(i, carry):
        yi, zi = lax.div(i, 4), lax.rem(i, 4)
        project(lk_wrap(y, yi), lk_wrap(z, zi), c)
        return carry

    def lk_wrap(base, offset):
        return lax.rem(base + offset, 4)

    lax.fori_loop(1, 16, project_own, 0)
    for copy in shared:
        copy.wait_recv()

    def project_sib(i, carry):
        yi, zi = lax.div(i, 4), lax.rem(i, 4)
        project(lk_wrap(y, yi), lk_wrap(z, zi), 1 - c)
        return carry

    lax.fori_loop(1, 16, project_sib, 0)
    qb[...] = qf[...].astype(BF16)
    for copy in hand:
        copy.wait_recv()

    doc_row = docs[...]
    doc_col[...] = jnp.broadcast_to(doc_row.astype(F32), (128, L)).T
    for h in range(2):
        hs = slice(h * HD, (h + 1) * HD)
        for rb in (1, 0):
            rows, nk = slice(rb * 256, rb * 256 + 256), rb * 256 + 256
            kk = kvh[0].reshape(L, HD)[:nk]
            vv = kvh[1].reshape(L, HD)[:nk]
            qh, gh = qb[rows, hs], cot[rows, hs]
            ri = lax.broadcasted_iota(jnp.int32, (256, nk), 0) + rb * 256
            ci = lax.broadcasted_iota(jnp.int32, (256, nk), 1)
            same = doc_col[rows, 0:1] == doc_row[:, :nk].astype(F32)
            allowed = jnp.logical_and(same, ci <= ri)
            w = jnp.where(allowed, jnp.exp(nt(qh, kk) * scale), 0.0)
            probs = w * (1.0 / jnp.sum(w, axis=1, keepdims=True))
            pb = probs.astype(BF16)
            att[rows, hs] = nn(pb, vv).astype(BF16)
            da = nt(gh, vv)
            ds = probs * (da - jnp.sum(da * probs, axis=1, keepdims=True)) * scale
            ds = ds.astype(BF16)
            dq[rows, hs] = nn(ds, kk).astype(BF16)
            dk_part, dv_part = tn(ds, qh), tn(pb, gh)
            if h == 0 and rb == 1:
                dkf[:nk, :HD] = dk_part
                dkf[:nk, HD:] = dv_part
            else:
                dkf[:nk, :HD] += dk_part
                dkf[:nk, HD:] += dv_part
    dkvp[...] = dkf[...].astype(BF16).reshape(4, 128, 256)

    sib_dq = lk.send(dq, dqs, sibling)
    quarter = 2 * zp + c
    swaps = []
    for i, (dev, qi) in enumerate(
        ((sibling, 2 * zp + 1 - c), (mate, 2 * (1 - zp) + c), (cross, 2 * (1 - zp) + 1 - c))
    ):
        swaps.append(lk.send(dkvp.at[qi], dkvt.at[i], dev))
    dqt[...] = dq[...].astype(F32).T.astype(BF16)

    rings = []

    def grad_query_group(j):
        for i in range(4):
            t = 4 * j + i
            part = nn(dqt[...], g[t // 8, (t // 2) % 4, t % 2]).astype(BF16)
            gq[j, :, :, i * 256 : (i + 1) * 256] = part.reshape(4, BLK, 256)
        rings.append(RingSum(lk, gq.at[j], gqr.at[j], gqf.at[j], gqo.at[j], 1 - 2 * (j % 2)))

    grad_query_group(0)
    grad_query_group(1)
    for copy in swaps:
        copy.wait_recv()
    total = dkvp[quarter].astype(F32)
    for i in range(3):
        total = total + dkvt[i].astype(F32)
    dkv[y, z, c] = total.astype(BF16)
    shared2 = [lk.send(dkv.at[y, z, c], dkv.at[y, z, c], sibling)]
    da_ = gather_half(lk, dkv, 0, 128, shared2)
    db_ = gather_half(lk, dkv, 1, 128, shared2)
    drive((da_, db_), 2)
    grad_query_group(2)
    grad_query_group(3)
    grad_query_group(4)
    drive((da_, db_), 2)
    grad_query_group(5)
    grad_query_group(6)
    grad_query_group(7)
    drive((da_, db_), 1)

    sib_mq.wait_recv()
    sib_dq.wait_recv()

    def dx_slot(yi, zi):
        part = nt(dq[...], mq[yi, zi, c]) + nt(dqs[...], mqs[yi, zi])
        dx[yi, zi] = part.astype(BF16)

    def dx_far_z(i, carry):
        dx_slot(i, lk_wrap(z, 2))
        return carry

    def dx_far_y(i, carry):
        dx_slot(lk_wrap(y, 2), lk_wrap(z, 2 + i))
        return carry

    def dx_near(i, carry):
        dx_slot(lk_wrap(y, 3 + lax.div(i, 3)), lk_wrap(z, 3 + lax.rem(i, 3)))
        return carry

    def store_dx(base, n, value):
        rows = slice(base, base + n)
        gtok[rows, :] = (value + dxkv[rows, :]).astype(BF16)

    xa = scatter_half(lk, dx, 0, L, dxt1, dxt2, dxt3, dxt4, store_dx)
    xb = scatter_half(lk, dx, 1, L, dxt1, dxt2, dxt3, dxt4, store_dx)
    lax.fori_loop(0, 4, dx_far_z, 0)
    drive((xa,))
    lax.fori_loop(1, 4, dx_far_y, 0)
    drive((xb,))
    lax.fori_loop(0, 9, dx_near, 0)
    drive((da_, db_), 4)
    drive((xa, xb))
    drive((da_, db_), 4)
    drive((xa, xb))
    rings[0].relay()
    rings[1].relay()
    finish((da_, db_))
    for copy in shared2:
        copy.wait_recv()

    for p in range(4):
        for hh in range(2):
            zi = 2 * hh
            pair = jnp.concatenate(
                [dkv[p, zi, 0], dkv[p, zi, 1], dkv[p, zi + 1, 0], dkv[p, zi + 1, 1]], axis=0
            )
            part = nn(tokt[...], pair).astype(BF16)
            gkv[0, p, :, hh * HD : (hh + 1) * HD] = part[:, :HD]
            gkv[1, p, :, hh * HD : (hh + 1) * HD] = part[:, HD:]
            more = nt(pair, mkv[2 * p + hh])
            if p == 0 and hh == 0:
                dxkv[...] = more
            else:
                dxkv[...] += more
    kv_rings = [
        RingSum(lk, gkv.at[i], gkvr.at[i], gkvf.at[i], gkvo.at[i], 1 - 2 * i) for i in range(2)
    ]
    for ring in rings[2:4]:
        ring.relay()
    drive((xa, xb))
    for ring in rings[4:6]:
        ring.relay()
    drive((xa, xb))
    for ring in rings[6:8]:
        ring.relay()
    finish((xa, xb))
    for ring in kv_rings:
        ring.relay()
    for j, ring in enumerate(rings):
        turned = ring.result().T
        for b in range(16):
            line = mrow[16 * j + b : 16 * j + b + 1, :BLK]
            rows = slice(j * 1024 + b * BLK, j * 1024 + (b + 1) * BLK)
            gq_out[rows, :] = (turned[b * BLK : (b + 1) * BLK, :] * line).astype(BF16)
    lane = lax.div(lax.broadcasted_iota(jnp.int32, (4, 256), 1), BLK)
    col = lax.broadcasted_iota(jnp.int32, (4, 16), 1)
    for ring, m, out in ((kv_rings[0], mask_k, gk_out), (kv_rings[1], mask_v, gv_out)):
        wide = jnp.zeros((4, 256), F32)
        for j in range(4):
            pick = jnp.sum(jnp.where(col == 4 * s + j, m[...].astype(F32), 0.0), axis=1, keepdims=True)
            wide = jnp.where(lane == j, pick, wide)
        total = ring.result()
        for b in range(4):
            rows = slice(b * BLK, (b + 1) * BLK)
            out[rows, :] = (total[rows, :] * wide[b : b + 1, :]).astype(BF16)
    lk.drain()


def on_device(tokens, cotangent, w_query, w_key, w_value, mask_query, mask_key, mask_value, documents):
    vmem = pl.BlockSpec(memory_space=pltpu.VMEM)
    any_space = pl.BlockSpec(memory_space=pl.ANY)
    dma = pltpu.SemaphoreType.DMA
    scratch = [
        ((4, 4, 2, 512, 256), BF16),
        ((4, 4, 2, 256, 256), BF16),
        ((4, 4, 256, 256), BF16),
        ((8, 256, 256), BF16),
        ((2, 256, 1024), BF16),
        ((256, 1024), BF16),
        ((128, 256), F32),
        ((128, 128), F32),
        ((512, 256), F32),
        ((512, 256), BF16),
        ((4, 4, 256, 128), BF16),
        ((2, 2, 4, 64, 128), BF16),
        ((2, 2, 4, 128, 128), BF16),
        ((2, 2, 64, 128), BF16),
        ((2, 2, 128, 128), BF16),
        ((2, 2, 256, 128), BF16),
        ((512, 128), F32),
        ((512, 256), F32),
        ((512, 256), BF16),
        ((512, 256), BF16),
        ((256, 512), BF16),
        ((256, 512), BF16),
        ((4, 128, 256), BF16),
        ((3, 128, 256), BF16),
        ((4, 4, 2, 128, 256), BF16),
        ((4, 4, 512, 256), BF16),
        ((2, 2, 4, 128, 256), BF16),
        ((2, 2, 4, 256, 256), BF16),
        ((2, 2, 128, 256), BF16),
        ((2, 2, 256, 256), BF16),
        ((512, 256), F32),
        ((8, 4, 64, 1024), BF16),
        ((8, 64, 1024), BF16),
        ((8, 64, 1024), BF16),
        ((8, 64, 1024), BF16),
        ((2, 4, 256, 256), BF16),
        ((2, 256, 256), BF16),
        ((2, 256, 256), BF16),
        ((2, 256, 256), BF16),
    ]
    return pl.pallas_call(
        kernel,
        name="step",
        out_shape=(
            jax.ShapeDtypeStruct((512, 256), BF16),
            jax.ShapeDtypeStruct((512, 256), BF16),
            jax.ShapeDtypeStruct((8192, 64), BF16),
            jax.ShapeDtypeStruct((256, 256), BF16),
            jax.ShapeDtypeStruct((256, 256), BF16),
        ),
        in_specs=[vmem, vmem, any_space] + [vmem] * 6,
        out_specs=(vmem,) * 5,
        scratch_shapes=[pltpu.VMEM(shape, dtype) for shape, dtype in scratch]
        + [dma((N_SEMS,)), dma((N_SEMS,)), dma],
        compiler_params=pltpu.CompilerParams(
            collective_id=0, has_side_effects=True, vmem_limit_bytes=67043328
        ),
    )(
        tokens, cotangent, w_query.reshape(4, 4, 2, 256, 256), w_key, w_value,
        mask_query, mask_key, mask_value, documents,
    )


def solution(mesh):
    in_specs = (
        P("seq", "tp"),
        P("seq", "tp"),
        P(None, "tp"),
        P("tp", None),
        P("tp", None),
        P(None, "tp"),
        P("tp", None),
        P("tp", None),
        P("seq", None),
    )
    out_specs = (
        P("seq", "tp"),
        P("seq", "tp"),
        P(None, ("tp", "seq")),
        P("tp", "seq"),
        P("tp", "seq"),
    )
    return jax.shard_map(
        on_device, mesh=mesh, in_specs=in_specs, out_specs=out_specs, check_vma=False
    )
```

time: 512 us -> 127 us (0.25)
  waiting for transfers between devices: 420 us -> 0 us
  Pallas kernels: 0 us -> 117 us
  matrix products: 45.2 us -> 0 us
  local copies, waits for them, and re-layouts: 23.3 us -> 8.8 us
  between operations: 14.4 us -> 0.66 us
  other arithmetic: 7.43 us -> 0 us
    psum x2 -> x0, waiting for transfers between devices: 205 us -> none  [the longest x1 107 us: on_device(): lax.psum(placed.astype(jnp.bfloat16), 'tp').astype(jnp.float32)]
    reduce_scatter x4 -> x0, waiting for transfers between devices: 157 us -> none  [the longest x1 95.2 us: on_device(): lax.psum_scatter(lax.dot_general(mq, d_query, (((1,), (1,)), ((), ())), p...]
    pallas_call x0 -> x1, Pallas kernels: none -> 117 us  [on_device(): pl.pallas_call(kernel, name='step', out_shape=(jax.ShapeDtypeStruct((512,...]
    all_gather x1 -> x0, waiting for transfers between devices: 57.4 us -> none  [on_device(): gathered = lax.all_gather(tokens, 'tp', axis=1, tiled=True)]
    dot_general x12 -> x0, matrix products: 45.2 us -> none  [the longest x1 7.83 us: on_device(): lax.dot_general(gathered, d_query, (((0,), (0,)), ((), ())), preferred_el...]
    unnamed x41 -> x9, local copies, waits for them, and re-layouts: 19.3 us -> 6.07 us
  transfers between devices with their start and end apart: 7 -> 0, of which waited for: 6 -> 0; matrix products, arithmetic and copies ran while one was open for 9% -> 0% of each run, Pallas kernels for 0% -> 0%
where the time goes in v1:
time: 127 us
  Pallas kernels  117 us (92%)
  local copies, waits for them, and re-layouts  8.8 us (7%)
    pallas_call x1, Pallas kernels, on_device(): pl.pallas_call(kernel, name='step', out_shape=(jax.ShapeDtypeStruct((512,...  117 us
    unnamed x9, local copies, waits for them, and re-layouts  6.07 us
    pallas_call x1, local copies, waits for them, and re-layouts, on_device(): pl.pallas_call(kernel, name='step', out_shape=(jax.ShapeDtypeStruct((512,...  2.73 us

profile of v1, /device:TPU:1, one launch (start us, length us, event | category | flops | bytes accessed | tf_op | source)
XLA Modules:
  0.0 126.6 jit_solution(14356754887696900769)
XLA Ops:
  0.6 1.4 %copy.14.mask_q = s32[128,4]{1,0:T(8,128)} copy(s32[128,4]{0,1:T(4,128)} %param.14) | data formatting | bytes 4096 | tf_op args[5]
  2.0 117.1 %step.1 = (bf16[512,256]{1,0:T(8,128)(2,1)}, bf16[512,256]{1,0:T(8,128)(2,1)}, bf16[8192,64]{1,0:T(8,128)(2,1)}, bf16[256,256]{1,0:T(8,128)(2,1)}, bf16[256,256]{1,0:T(8,128)(2,1)}) custom-call(bf16[512,256]{1,0:T(8,128)(2,1)} %tok.1, bf16[512,256]{1,0:T(8,128)(2,1)} %cot.1, bf16[4,4,2,256,256]{4,3,2,1,0:T(8,128)(2,1)} %bitcast.1, bf16[256,1024]{1,0:T(8,128)(2,1)} %wk.1, ...), custom_call_target="tpu_custom_call" | custom-call | tf_op jit(solution)/shard_map/step/pallas_call | solution.py:563
  119.1 0.0 copy-start.1
  119.2 0.0 copy-start
  119.2 2.7 %copy.15 = bf16[8192,64]{0,1:T(8,128)(2,1)} copy(bf16[8192,64]{1,0:T(8,128)(2,1)} %get-tuple-element.7) | data formatting | bytes 2097152 | tf_op jit(solution)/shard_map/step/pallas_call | solution.py:563
  121.9 1.7 %copy.20 = bf16[512,256]{1,0:T(8,128)(2,1)} copy(bf16[512,256]{1,0:T(8,128)(2,1)} %get-tuple-element.15) | data formatting | bytes 524288
  123.6 1.7 %copy.21 = bf16[512,256]{1,0:T(8,128)(2,1)} copy(bf16[512,256]{1,0:T(8,128)(2,1)} %get-tuple-element.16) | data formatting | bytes 524288
  125.2 0.0 copy-done.1
  125.2 0.7 copy.22
  125.9 0.0 copy-done
  125.9 0.7 copy.23
Async XLA Ops:
  119.1 6.1 %copy-start.1 = (bf16[256,256]{1,0:T(8,128)(2,1)S(1)}, bf16[256,256]{1,0:T(8,128)(2,1)}, u32[]{:S(2)}) copy-start(bf16[256,256]{1,0:T(8,128)(2,1)} %get-tuple-element.18) | copy-start | bytes 393220
  119.2 6.7 %copy-start = (bf16[256,256]{1,0:T(8,128)(2,1)S(1)}, bf16[256,256]{1,0:T(8,128)(2,1)}, u32[]{:S(2)}) copy-start(bf16[256,256]{1,0:T(8,128)(2,1)} %get-tuple-element.19) | copy-start | bytes 393220

commit v2 on v1

--- a/solution.py
+++ b/solution.py
@@ -278,13 +278,24 @@
     drive((ga, gb), 2)
 
     lane = lax.div(lax.broadcasted_iota(jnp.int32, (128, 256), 1), BLK)
-    col = lax.broadcasted_iota(jnp.int32, (128, 4), 1)
+    row = lax.broadcasted_iota(jnp.int32, (128, 128), 0)
+    cols = jnp.zeros((128, 128), F32)
+    own = jnp.zeros((8, 128), F32)
+    for j in range(4):
+        line = mask_q[j : j + 1, :].astype(F32)
+        cols = jnp.where(row == j, line, cols)
+        own = jnp.where(s == j, line, own)
+    cols = cols.T
     wide = jnp.zeros((128, 256), F32)
     for j in range(4):
-        wide = jnp.where(lane == j, mask_q[:, j : j + 1].astype(F32), wide)
+        wide = jnp.where(lane == j, cols[:, j : j + 1], wide)
     mexp[...] = wide
-    own_col = jnp.sum(jnp.where(col == s, mask_q[...].astype(F32), 0.0), axis=1, keepdims=True)
-    mrow[...] = jnp.broadcast_to(own_col, (128, 128))
+    own = own.astype(BF16)
+    ahead = lax.broadcasted_iota(jnp.int32, (128, 1024), 0) - lax.div(
+        lax.broadcasted_iota(jnp.int32, (128, 1024), 1), BLK
+    )
+    for j in range(8):
+        mrow[:, j * 1024 : (j + 1) * 1024] = nn(own, jnp.where(ahead == 16 * j, 1.0, 0.0).astype(BF16))
     weights.wait()
 
     def mask_chunk(t, carry):
@@ -496,11 +507,8 @@
     for ring in kv_rings:
         ring.relay()
     for j, ring in enumerate(rings):
-        turned = ring.result().T
-        for b in range(16):
-            line = mrow[16 * j + b : 16 * j + b + 1, :BLK]
-            rows = slice(j * 1024 + b * BLK, j * 1024 + (b + 1) * BLK)
-            gq_out[rows, :] = (turned[b * BLK : (b + 1) * BLK, :] * line).astype(BF16)
+        cols = slice(j * 1024, (j + 1) * 1024)
+        gq_out[:, cols] = (ring.result() * mrow[0:1, cols]).astype(BF16)
     lane = lax.div(lax.broadcasted_iota(jnp.int32, (4, 256), 1), BLK)
     col = lax.broadcasted_iota(jnp.int32, (4, 16), 1)
     for ring, m, out in ((kv_rings[0], mask_k, gk_out), (kv_rings[1], mask_v, gv_out)):
@@ -527,7 +535,7 @@
         ((2, 256, 1024), BF16),
         ((256, 1024), BF16),
         ((128, 256), F32),
-        ((128, 128), F32),
+        ((8, 8192), F32),
         ((512, 256), F32),
         ((512, 256), BF16),
         ((4, 4, 256, 128), BF16),
@@ -560,13 +568,13 @@
         ((2, 256, 256), BF16),
         ((2, 256, 256), BF16),
     ]
-    return pl.pallas_call(
+    att, gtok, gq, gk, gv = pl.pallas_call(
         kernel,
         name="step",
         out_shape=(
             jax.ShapeDtypeStruct((512, 256), BF16),
             jax.ShapeDtypeStruct((512, 256), BF16),
-            jax.ShapeDtypeStruct((8192, 64), BF16),
+            jax.ShapeDtypeStruct((64, 8192), BF16),
             jax.ShapeDtypeStruct((256, 256), BF16),
             jax.ShapeDtypeStruct((256, 256), BF16),
         ),
@@ -579,8 +587,47 @@
         ),
     )(
         tokens, cotangent, w_query.reshape(4, 4, 2, 256, 256), w_key, w_value,
-        mask_query, mask_key, mask_value, documents,
+        mask_query.T, mask_key, mask_value, documents,
     )
+    att, gtok, gq, gk, gv = hand_out(att, gtok, gq, gk, gv)
+    return att, gtok, gq.T, gk, gv
+
+
+def hand_out_kernel(*refs):
+    srcs, dsts, bufs, in_sem, out_sem = refs[:5], refs[5:10], refs[10:15], refs[15], refs[16]
+    pieces = []
+    for src, dst, buf in zip(srcs, dsts, bufs):
+        n = max(1, src.shape[1] // 4096)
+        w = src.shape[1] // n
+        for i in range(n):
+            cols = pl.ds(i * w, w)
+            pieces.append((src.at[:, cols], buf.at[:, cols], dst.at[:, cols]))
+    fetches = [
+        pltpu.make_async_copy(src, buf, in_sem.at[i]) for i, (src, buf, _) in enumerate(pieces)
+    ]
+    puts = [
+        pltpu.make_async_copy(buf, dst, out_sem.at[i]) for i, (_, buf, dst) in enumerate(pieces)
+    ]
+    for fetch in fetches:
+        fetch.start()
+    for fetch, put in zip(fetches, puts):
+        fetch.wait()
+        put.start()
+    for put in puts:
+        put.wait()
+
+
+def hand_out(*arrays):
+    any_space = pl.BlockSpec(memory_space=pl.ANY)
+    return pl.pallas_call(
+        hand_out_kernel,
+        name="hand_out",
+        out_shape=tuple(jax.ShapeDtypeStruct(a.shape, a.dtype) for a in arrays),
+        in_specs=[any_space] * 5,
+        out_specs=(any_space,) * 5,
+        scratch_shapes=[pltpu.VMEM(a.shape, a.dtype) for a in arrays]
+        + [pltpu.SemaphoreType.DMA((6,)), pltpu.SemaphoreType.DMA((6,))],
+    )(*arrays)
 
 
 def solution(mesh):

time: 127 us -> 120 us (0.945)
  local copies, waits for them, and re-layouts: 8.8 us -> 0 us
  Pallas kernels: 117 us -> 119 us
    unnamed x9 -> x0, local copies, waits for them, and re-layouts: 6.07 us -> none
    pallas_call x1 -> x0, local copies, waits for them, and re-layouts: 2.73 us -> none  [on_device(): pl.pallas_call(kernel, name='step', out_shape=(jax.ShapeDtypeStruct((512,...]
    pallas_call x0 -> x1, Pallas kernels: none -> 2.35 us  [hand_out(): pl.pallas_call(hand_out_kernel, name='hand_out', out_shape=tuple((jax.Sha...]
where the time goes in v2:
time: 120 us
  Pallas kernels  119 us (99%)
    pallas_call x1, Pallas kernels, on_device(): pl.pallas_call(kernel, name='step', out_shape=(jax.ShapeDtypeStruct((512,...  117 us

profile of v2, /device:TPU:1, one launch (start us, length us, event | category | flops | bytes accessed | tf_op | source)
XLA Modules:
  0.0 119.9 jit_solution(8769705694567126049)
XLA Ops:
  0.6 116.9 %step.1 = (bf16[512,256]{1,0:T(8,128)(2,1)}, bf16[512,256]{1,0:T(8,128)(2,1)}, bf16[64,8192]{1,0:T(8,128)(2,1)}, bf16[256,256]{1,0:T(8,128)(2,1)}, bf16[256,256]{1,0:T(8,128)(2,1)}) custom-call(bf16[512,256]{1,0:T(8,128)(2,1)} %tok.1, bf16[512,256]{1,0:T(8,128)(2,1)} %cot.1, bf16[4,4,2,256,256]{4,3,2,1,0:T(8,128)(2,1)} %bitcast.3, bf16[256,1024]{1,0:T(8,128)(2,1)} %wk.1, ...), custom_call_target="tpu_custom_call" | custom-call | tf_op jit(solution)/shard_map/step/pallas_call | solution.py:571
  117.5 2.4 %hand_out.1 = (bf16[512,256]{1,0:T(8,128)(2,1)}, bf16[512,256]{1,0:T(8,128)(2,1)}, bf16[64,8192]{1,0:T(8,128)(2,1)}, bf16[256,256]{1,0:T(8,128)(2,1)}, bf16[256,256]{1,0:T(8,128)(2,1)}) custom-call(bf16[512,256]{1,0:T(8,128)(2,1)} %get-tuple-element.15.refs_0_, bf16[512,256]{1,0:T(8,128)(2,1)} %get-tuple-element.16.refs_1_, ...), custom_call_target="tpu_custom_call" | custom-call | tf_op jit(solution)/shard_map/hand_out/pallas_call | solution.py:622

commit v3 on v2

--- a/solution.py
+++ b/solution.py
@@ -431,12 +431,7 @@
     drive((da_, db_), 2)
     grad_query_group(2)
     grad_query_group(3)
-    grad_query_group(4)
     drive((da_, db_), 2)
-    grad_query_group(5)
-    grad_query_group(6)
-    grad_query_group(7)
-    drive((da_, db_), 1)
 
     sib_mq.wait_recv()
     sib_dq.wait_recv()
@@ -467,6 +462,11 @@
     drive((xa,))
     lax.fori_loop(1, 4, dx_far_y, 0)
     drive((xb,))
+    grad_query_group(4)
+    grad_query_group(5)
+    drive((da_, db_), 1)
+    grad_query_group(6)
+    grad_query_group(7)
     lax.fori_loop(0, 9, dx_near, 0)
     drive((da_, db_), 4)
     drive((xa, xb))

time: 120 us -> 117 us (0.975)
  Pallas kernels: 119 us -> 116 us
    pallas_call x1, Pallas kernels: 117 us -> 114 us  [on_device(): pl.pallas_call(kernel, name='step', out_shape=(jax.ShapeDtypeStruct((512,...]
where the time goes in v3:
time: 117 us
  Pallas kernels  116 us (99%)
    pallas_call x1, Pallas kernels, on_device(): pl.pallas_call(kernel, name='step', out_shape=(jax.ShapeDtypeStruct((512,...  114 us
    pallas_call x1, Pallas kernels, hand_out(): pl.pallas_call(hand_out_kernel, name='hand_out', out_shape=tuple((jax.Sha...  2.35 us

profile of v3, /device:TPU:1, one launch (start us, length us, event | category | flops | bytes accessed | tf_op | source)
XLA Modules:
  0.0 117.2 jit_solution(17952089172888736408)
XLA Ops:
  0.6 114.1 %step.1 = (bf16[512,256]{1,0:T(8,128)(2,1)}, bf16[512,256]{1,0:T(8,128)(2,1)}, bf16[64,8192]{1,0:T(8,128)(2,1)}, bf16[256,256]{1,0:T(8,128)(2,1)}, bf16[256,256]{1,0:T(8,128)(2,1)}) custom-call(bf16[512,256]{1,0:T(8,128)(2,1)} %tok.1, bf16[512,256]{1,0:T(8,128)(2,1)} %cot.1, bf16[4,4,2,256,256]{4,3,2,1,0:T(8,128)(2,1)} %bitcast.3, bf16[256,1024]{1,0:T(8,128)(2,1)} %wk.1, ...), custom_call_target="tpu_custom_call" | custom-call | tf_op jit(solution)/shard_map/step/pallas_call | solution.py:571
  114.7 2.4 %hand_out.1 = (bf16[512,256]{1,0:T(8,128)(2,1)}, bf16[512,256]{1,0:T(8,128)(2,1)}, bf16[64,8192]{1,0:T(8,128)(2,1)}, bf16[256,256]{1,0:T(8,128)(2,1)}, bf16[256,256]{1,0:T(8,128)(2,1)}) custom-call(bf16[512,256]{1,0:T(8,128)(2,1)} %get-tuple-element.15.refs_0_, bf16[512,256]{1,0:T(8,128)(2,1)} %get-tuple-element.16.refs_1_, ...), custom_call_target="tpu_custom_call" | custom-call | tf_op jit(solution)/shard_map/hand_out/pallas_call | solution.py:622
